TPU v7x, 32 devices: a whole 2x2x4 slice. The times are simulated.
32 devices in a mesh: row: 4 (over y, x), col: 8 (over z, core).
Axes of the slice: x: 2, y: 2, z: 4, core: 2. Of those that a mesh axis runs over, the one named last changes fastest.
Arguments:
- parent_front: bfloat16 [28672, 28672], P('row', 'col'), may hold values from -6 to 6
- child_update: bfloat16 [2, 14336, 14336], P(None, 'row', 'col'), may hold values from -6 to 6
- parent_test: bfloat16 [28672, 448], P('col'), may hold values from -0.03125 to 0.03125
- child_test: bfloat16 [2, 14336, 448], P(None, 'col'), may hold values from -0.046875 to 0.046875
- child_map: int32 [2, 112], replicated, may hold values from 0 to 223, as said below
Outputs:
- leaf_basis: bfloat16 [224, 128, 448], P('row', 'col')
- couplings: float32 [32, 448, 448], P('row', 'col')
Inputs may be any that keep to these rules, and one draw needn't show every extreme that they name: `child_map`: for each child the entries rise strictly along its blocks, and entry j is at least j.
All inputs are finite; a program needn't handle non-finite values.
Results may differ from a plain program's by a relative error of at most 0.006.
Values may be sent and summed in bfloat16 or wider, within the bound.
A program may use at most 192 MiB of HBM per device.

v0:
```python
import math
import jax
import jax.numpy as jnp
from jax import lax
from jax.sharding import PartitionSpec as P

LEAF = 896
BLOCK = 128
HIGH = lax.Precision.HIGHEST


def spread(block, axis, holder):
    block = jnp.where(lax.axis_index(axis) == holder, block, jnp.zeros_like(block))
    return lax.psum(block, axis)


def finish(leaves, gram_matrix):
    factor = jnp.linalg.cholesky(gram_matrix)
    solved = lax.linalg.triangular_solve(
        factor, leaves, left_side=False, lower=True, transpose_a=True
    )
    return (solved * math.sqrt(LEAF)).astype(jnp.bfloat16)


def local(parent_front, child_update, parent_test, child_test, child_map):
    row_count = lax.axis_size("row")
    col_count = lax.axis_size("col")
    row_index = lax.axis_index("row")
    col_index = lax.axis_index("col")
    slab_rows = BLOCK // col_count
    own_blocks = parent_front.shape[0] // BLOCK
    kid_blocks = child_update.shape[1] // BLOCK
    probes = parent_test.shape[1]
    own_probe = jnp.dot(parent_front, parent_test, preferred_element_type=jnp.float32)
    own_probe = own_probe.reshape(own_blocks, BLOCK, probes)
    kid_probe = jnp.stack(
        [
            jnp.dot(child_update[which], child_test[which], preferred_element_type=jnp.float32)
            for which in range(2)
        ]
    )
    kid_probe = kid_probe.reshape(2, kid_blocks, BLOCK, probes)
    own_share, kid_share = (
        lax.psum_scatter(own_probe, "col", scatter_dimension=1, tiled=True),
        lax.psum_scatter(kid_probe, "col", scatter_dimension=2, tiled=True),
    )
    first_block = row_index * own_blocks
    targets = jnp.arange(own_blocks, dtype=jnp.int32)
    mapped = child_map - first_block
    onehot = (mapped[:, None, :] == targets[None, :, None]).astype(jnp.float32)
    sample = own_share + jnp.einsum(
        "cpn,cnsr->psr",
        onehot,
        lax.all_gather(kid_share, "row", axis=1, tiled=True),
        precision=HIGH,
    )
    per_leaf = LEAF // BLOCK
    leaf_count = own_blocks // per_leaf
    leaves = sample.reshape(leaf_count, per_leaf * slab_rows, probes)
    partial_gram = jnp.einsum("lkr,lks->lrs", leaves, leaves, precision=HIGH)
    gram_matrix = lax.psum(partial_gram, "col")
    leaf_basis = finish(leaves, gram_matrix).reshape(own_blocks, slab_rows, probes)
    whole_basis = lax.all_gather(leaf_basis, "col", axis=1, tiled=True)
    bases = whole_basis.reshape(leaf_count, LEAF, probes)
    col_leaves = parent_front.shape[1] // LEAF
    shrink = 1.0 / math.sqrt(LEAF)

    def sibling_product(position):
        leaf_index = col_index * col_leaves + position
        sibling = jnp.bitwise_xor(leaf_index, 1)
        row_start = leaf_index % leaf_count * LEAF
        col_start = (sibling - col_index * col_leaves) * LEAF
        front_tile = lax.dynamic_slice(parent_front, (row_start, col_start), (LEAF, LEAF))
        product = (
            jnp.dot(front_tile, bases[sibling % leaf_count], preferred_element_type=jnp.float32)
            * shrink
        )
        return product.astype(jnp.bfloat16)

    products = lax.map(sibling_product, jnp.arange(col_leaves, dtype=jnp.int32))
    owner_span = col_count // row_count
    core_rows = probes // col_count
    received = [
        spread(products, "col", row_index * owner_span + offset) for offset in range(owner_span)
    ]
    products_all = jnp.concatenate(received, axis=0)
    columns = lax.dynamic_slice_in_dim(bases, col_index * core_rows, core_rows, 2)
    couplings = (
        jnp.einsum("lkr,lks->lrs", columns, products_all, preferred_element_type=jnp.float32)
        * shrink
    )
    return (leaf_basis, couplings)


def solution(mesh):
    in_specs = (P("row", "col"), P(None, "row", "col"), P("col", None), P(None, "col", None), P())
    out_specs = (P("row", "col", None), P("row", "col", None))
    return jax.shard_map(local, mesh=mesh, in_specs=in_specs, out_specs=out_specs, check_vma=False)
```

profile of v0, /device:TPU:0, one launch (start us, length us, event | category | flops | bytes accessed | tf_op | source)
XLA Modules:
  0.0 1988.0 jit_solution(7997422557833170795)
XLA Ops:
  7.2 9.5 fusion.77
  16.7 10.6 convolution_bitcast_fusion.1
  27.3 10.6 convolution_bitcast_fusion.2
  37.8 10.9 pad_maximum_fusion
  48.7 21.7 %copy.91 = f32[2,28,128,448]{3,0,1,2:T(2,128)} copy(f32[2,28,128,448]{2,3,1,0:T(8,128)} %pad_maximum_fusion) | data formatting | bytes 25690112 | tf_op jit(solution)/shard_map/stack | solution.py:36
  72.3 295.1 %all-reduce.11.cloned.1.call-done = f32[2,28,128,448]{3,0,1,2:T(2,128)} async-done(((f32[2,28,128,448]{3,0,1,2:T(2,128)}), f32[2,28,128,448]{3,0,1,2:T(2,128)}) %all-reduce.11.cloned.1.call-update) | async-done | bytes 12845072
  372.4 30.3 %convolution_bitcast_fusion = f32[56,8,56,128]{3,1,2,0:T(8,128)} fusion(bf16[7168,3584]{1,0:T(8,128)(2,1)} %param.7, bf16[3584,448]{0,1:T(8,128)(2,1)S(1)} %copy-done), kind=kOutput, calls=%fused_computation.11 | convolution fusion | flops 23018340352 | bytes 67436544 | tf_op jit(solution)/shard_map/dot_general | solution.py:34
  402.7 12.1 copy.136
  414.8 16.4 copy.90
  431.9 19.0 all-gather.3.cloned.1.call-done
  450.9 151.3 %reduce-scatter.2.cloned.1.call-done = f32[56,16,448]{2,0,1:T(8,128)} async-done(((f32[56,128,448]{2,0,1:T(8,128)}), f32[56,16,448]{2,0,1:T(8,128)}) %reduce-scatter.2.cloned.1.call-update) | async-done | bytes 1605648 | tf_op jit(solution)/shard_map/reduce_scatter | solution.py:44
  602.2 10.3 bitcast_add_fusion.1
  613.6 8.1 fusion.78
  623.1 153.0 %all-reduce.9.cloned.1.call-done = f32[8,448,448]{1,2,0:T(8,128)} async-done(((f32[8,448,448]{1,2,0:T(8,128)}), f32[8,448,448]{1,2,0:T(8,128)}) %all-reduce.9.cloned.1.call-update) | async-done | bytes 6422544 | tf_op jit(solution)/shard_map/psum | solution.py:61
  776.1 8.5 copy.97
  784.6 7.0 fusion.13
  794.6 93.8 %custom-call.34 = f32[8,128,128]{2,1,0:T(8,128)S(1)} custom-call(f32[8,128,128]{2,1,0:T(8,128)S(1)} %cholesky.281), custom_call_target="Cholesky" | custom-call | tf_op jit(solution)/shard_map/jit(cholesky)/cholesky | solution.py:18
  888.4 4.0 cholesky.236
  892.4 79.2 %custom-call.35 = f32[8,1,128,128]{2,3,1,0:T(8,128)} custom-call(f32[8,1,128,128]{3,2,1,0:T(8,128)S(1)} %select_bitcast_fusion.2), custom_call_target="InvertDiagBlocksLowerTriangular" | custom-call | tf_op jit(solution)/shard_map/jit(cholesky)/cholesky | solution.py:18
  971.7 3.9 constant_dynamic-update-slice_fusion.3
  979.3 94.2 %custom-call.36 = f32[8,128,128]{2,1,0:T(8,128)S(1)} custom-call(f32[8,128,128]{2,1,0:T(8,128)S(1)} %cholesky.285), custom_call_target="Cholesky" | custom-call | tf_op jit(solution)/shard_map/jit(cholesky)/cholesky | solution.py:18
  1074.5 79.2 %custom-call.37 = f32[8,1,128,128]{2,3,1,0:T(8,128)} custom-call(f32[8,1,128,128]{3,2,1,0:T(8,128)S(1)} %get-tuple-element.154), custom_call_target="InvertDiagBlocksLowerTriangular" | custom-call | tf_op jit(solution)/shard_map/jit(cholesky)/cholesky | solution.py:18
  1161.3 95.4 %custom-call.38 = f32[8,128,128]{2,1,0:T(8,128)} custom-call(f32[8,128,128]{2,1,0:T(8,128)} %cholesky.290), custom_call_target="Cholesky" | custom-call | tf_op jit(solution)/shard_map/jit(cholesky)/cholesky | solution.py:18
  1259.1 79.4 %custom-call.39 = f32[8,1,128,128]{2,3,1,0:T(8,128)S(1)} custom-call(f32[8,1,128,128]{3,2,1,0:T(8,128)} %get-tuple-element.152), custom_call_target="InvertDiagBlocksLowerTriangular" | custom-call | tf_op jit(solution)/shard_map/jit(cholesky)/cholesky | solution.py:18
  1342.4 46.9 %custom-call.40 = f32[8,64,64]{2,1,0:T(8,128)S(1)} custom-call(f32[8,64,64]{2,1,0:T(8,128)S(1)} %convolution_subtract_fusion.3), custom_call_target="Cholesky" | custom-call | tf_op jit(solution)/shard_map/jit(cholesky)/cholesky | solution.py:18
  1390.4 4.3 select_select_fusion
  1397.7 12.5 while.16
  1413.5 316.0 %custom-call.41 = f32[8,4,128,128]{2,3,1,0:T(8,128)} custom-call(f32[8,4,128,128]{3,2,1,0:T(8,128)} %pad_maximum_fusion.1), custom_call_target="InvertDiagBlocksLowerTriangular" | custom-call | tf_op jit(solution)/shard_map/triangular_solve | solution.py:19
  1742.5 73.5 %all-gather.5.cloned.1.call-done = bf16[56,128,448]{2,1,0:T(8,128)(2,1)} async-done(((bf16[56,16,448]{2,1,0:T(8,128)(2,1)}), bf16[56,128,448]{2,1,0:T(8,128)(2,1)}) %all-gather.5.cloned.1.call-update) | async-done | bytes 6422544 | tf_op jit(solution)/shard_map/all_gather | solution.py:63
  1816.0 17.0 while.15
  1836.2 137.2 %all-reduce.13.cloned.1.call-done = (bf16[4,896,448]{1,2,0:T(8,128)(2,1)}, bf16[4,896,448]{1,2,0:T(8,128)(2,1)}) async-done(((bf16[4,896,448]{1,2,0:T(8,128)(2,1)}, bf16[4,896,448]{1,2,0:T(8,128)(2,1)}), (bf16[4,896,448]{1,2,0:T(8,128)(2,1)}, bf16[4,896,448]{1,2,0:T(8,128)(2,1)})) %all-reduce.13.cloned.1.call-update) | async-done | bytes 6422544 | tf_op jit(solution)/shard_map/psum | solution.py:14
  1973.5 7.4 fusion.52
  (98 shorter events, 80.9 us)
Async XLA Ops:
  7.2 365.2 %copy-start = (bf16[3584,448]{0,1:T(8,128)(2,1)S(1)}, bf16[3584,448]{0,1:T(8,128)(2,1)}, u32[]{:S(2)}) copy-start(bf16[3584,448]{0,1:T(8,128)(2,1)} %param.9) | copy-start | bytes 9633796
  7.2 360.2 %all-reduce.11.cloned.1.call-start = ((), (), s32[]{:S(2)}) async-start(), calls=%async_computation.5 | async-start | bytes 29360128
  70.4 0.7 copy-start.10
  70.4 380.5 %all-gather.3.cloned.1.call-start = ((), (), s32[]{:S(2)}) async-start(), calls=%async_computation.2 | async-start | bytes 9175040 | tf_op jit(solution)/shard_map/all_gather | solution.py:54
  371.8 230.4 %reduce-scatter.2.cloned.1.call-start = ((), (), s32[]{:S(2)}) async-start(), calls=%async_computation.1 | async-start | bytes 16515072 | tf_op jit(solution)/shard_map/reduce_scatter | solution.py:44
  431.2 0.7 copy-start.9
  431.2 344.9 %all-reduce.9.cloned.1.call-start = ((), (), s32[]{:S(2)}) async-start(), calls=%async_computation.3 | async-start | bytes 14680064 | tf_op jit(solution)/shard_map/psum | solution.py:61
  621.7 1194.3 %all-gather.5.cloned.1.call-start = ((), (), s32[]{:S(2)}) async-start(), calls=%async_computation.4 | async-start | bytes 8257536 | tf_op jit(solution)/shard_map/all_gather | solution.py:63
  791.6 2.9 copy-start.3
  888.4 4.0 copy-start.5
  978.2 1.1 copy-start.4
  1073.5 80.2 %copy-start.7 = (f32[8,128,128]{2,1,0:T(8,128)}, f32[8,128,128]{2,1,0:T(8,128)S(1)}, u32[]{:S(2)}) copy-start(f32[8,128,128]{2,1,0:T(8,128)S(1)} %custom-call.36) | copy-start | bytes 1572868
  1153.8 102.9 %copy-start.6 = (f32[8,128,128]{2,1,0:T(8,128)S(1)}, f32[8,128,128]{2,1,0:T(8,128)}, u32[]{:S(2)}) copy-start(f32[8,128,128]{2,1,0:T(8,128)} %copy-done.5) | copy-start | bytes 1572868
  1394.7 2.9 copy-start.2
  1729.5 4.1 copy-start.8
  1742.4 231.1 %all-reduce.13.cloned.1.call-start = ((), (), s32[]{:S(2)}) async-start(), calls=%async_computation.6 | async-start | bytes 12845056 | tf_op jit(solution)/shard_map/psum | solution.py:14
  1973.5 7.4 copy-start.1
Sparse Core Ops, SparseCore 0:
  70.5 296.7 all-reduce.10
  371.9 78.9 all-gather.2
  453.2 148.9 reduce-scatter.1
  621.9 154.2 all-reduce.8
  1742.5 73.4 all-gather.4
  1836.3 137.0 all-reduce.12
where the time goes:
time: 2000 us; the launch traced here: 1990 us
  other arithmetic  919 us (46%)
  waiting for transfers between devices  829 us (41%)
  matrix products  118 us (6%)
  local copies, waits for them, and re-layouts  102 us (5%)
    another operation x18, other arithmetic, finish(): factor = jnp.linalg.cholesky(gram_matrix)  573 us
    another operation x8, other arithmetic, finish(): lax.linalg.triangular_solve(factor, leaves, left_side=False, lower=True,...  324 us
    unnamed x7, waiting for transfers between devices  295 us
    psum x1, waiting for transfers between devices, local(): gram_matrix = lax.psum(partial_gram, 'col')  153 us
    reduce_scatter x1, waiting for transfers between devices, local(): lax.psum_scatter(own_probe, 'col', scatter_dimension=1, tiled=True)  151 us
    psum x1, waiting for transfers between devices, spread(): return lax.psum(block, axis)  137 us
    all_gather x1, waiting for transfers between devices, local(): whole_basis = lax.all_gather(leaf_basis, 'col', axis=1, tiled=True)  73.5 us
  transfers between devices with their start and end apart: 6, of which 6 were waited for; matrix products, arithmetic and copies ran while one was open for 3% of the time, Pallas kernels for 0%

commit v1 on v0

--- a/solution.py
+++ b/solution.py
@@ -58,7 +58,11 @@
     leaf_count = own_blocks // per_leaf
     leaves = sample.reshape(leaf_count, per_leaf * slab_rows, probes)
     partial_gram = jnp.einsum("lkr,lks->lrs", leaves, leaves, precision=HIGH)
-    gram_matrix = lax.psum(partial_gram, "col")
+    gram_matrix = partial_gram
+    for hop in (1, 2, 4):
+        gram_matrix = gram_matrix + lax.ppermute(
+            gram_matrix, "col", [(dev, dev ^ hop) for dev in range(8)]
+        )
     leaf_basis = finish(leaves, gram_matrix).reshape(own_blocks, slab_rows, probes)
     whole_basis = lax.all_gather(leaf_basis, "col", axis=1, tiled=True)
     bases = whole_basis.reshape(leaf_count, LEAF, probes)

time: 2000 us -> 2350 us (1.18)
  waiting for transfers between devices: 829 us -> 1160 us
  other arithmetic: 919 us -> 945 us
    ppermute x0 -> x3, waiting for transfers between devices: none -> 488 us  [local(): lax.ppermute(gram_matrix, 'col', [(dev, dev ^ hop) for dev in range(8)])]
    psum x1 -> x0, waiting for transfers between devices: 153 us -> none  [local(): gram_matrix = lax.psum(partial_gram, 'col')]
    add x0 -> x3, other arithmetic: none -> 25.8 us  [local(): gram_matrix + lax.ppermute(gram_matrix, 'col', [(dev, dev ^ hop) for dev...]
    unnamed x7 -> x6, waiting for transfers between devices: 295 us -> 295 us
  transfers between devices with their start and end apart: 6 -> 8, of which waited for: 6 -> 8; matrix products, arithmetic and copies ran while one was open for 3% -> 3% of each run, Pallas kernels for 0% -> 0%
where the time goes in v1:
time: 2350 us
  waiting for transfers between devices  1160 us (49%)
  other arithmetic  945 us (40%)
  matrix products  116 us (5%)
  local copies, waits for them, and re-layouts  103 us (4%)
    another operation x18, other arithmetic, finish(): factor = jnp.linalg.cholesky(gram_matrix)  572 us
    ppermute x3, waiting for transfers between devices, local(): lax.ppermute(gram_matrix, 'col', [(dev, dev ^ hop) for dev in range(8)])  488 us
    another operation x8, other arithmetic, finish(): lax.linalg.triangular_solve(factor, leaves, left_side=False, lower=True,...  324 us
    unnamed x6, waiting for transfers between devices  295 us
    reduce_scatter x1, waiting for transfers between devices, local(): lax.psum_scatter(own_probe, 'col', scatter_dimension=1, tiled=True)  151 us
    psum x1, waiting for transfers between devices, spread(): return lax.psum(block, axis)  137 us
    all_gather x1, waiting for transfers between devices, local(): whole_basis = lax.all_gather(leaf_basis, 'col', axis=1, tiled=True)  71.9 us
  transfers between devices with their start and end apart: 8, of which 8 were waited for; matrix products, arithmetic and copies ran while one was open for 3% of the time, Pallas kernels for 0%

profile of v1, /device:TPU:0, one launch (start us, length us, event | category | flops | bytes accessed | tf_op | source)
XLA Modules:
  0.0 2346.2 jit_solution(4448638083707613202)
XLA Ops:
  7.2 9.5 fusion.78
  16.7 10.6 convolution_bitcast_fusion.1
  27.3 10.5 convolution_bitcast_fusion.2
  37.9 10.9 pad_maximum_fusion
  48.7 21.7 copy.95
  72.3 295.1 %all-reduce.8.cloned.1.call-done = f32[2,28,128,448]{3,0,1,2:T(2,128)} async-done(((f32[2,28,128,448]{3,0,1,2:T(2,128)}), f32[2,28,128,448]{3,0,1,2:T(2,128)}) %all-reduce.8.cloned.1.call-update) | async-done | bytes 12845072
  372.4 30.3 %convolution_bitcast_fusion = f32[56,8,56,128]{3,1,2,0:T(8,128)} fusion(bf16[7168,3584]{1,0:T(8,128)(2,1)} %param.7, bf16[3584,448]{0,1:T(8,128)(2,1)S(1)} %copy-done), kind=kOutput, calls=%fused_computation.11 | convolution fusion | flops 23018340352 | bytes 67436544 | tf_op jit(solution)/shard_map/dot_general | solution.py:34
  402.7 12.1 copy.141
  414.8 16.4 copy.94
  431.9 19.0 all-gather.3.cloned.1.call-done
  450.9 151.3 %reduce-scatter.2.cloned.1.call-done = f32[56,16,448]{2,0,1:T(8,128)} async-done(((f32[56,128,448]{2,0,1:T(8,128)}), f32[56,16,448]{2,0,1:T(8,128)}) %reduce-scatter.2.cloned.1.call-update) | async-done | bytes 1605648 | tf_op jit(solution)/shard_map/reduce_scatter | solution.py:44
  602.2 10.3 bitcast_add_fusion.1
  619.9 11.8 collective-permute-done
  631.7 7.9 add.112
  639.6 160.2 %collective-permute-done.1 = f32[8,448,448]{1,2,0:T(8,128)S(1)} collective-permute-done((f32[8,448,448]{1,2,0:T(8,128)}, f32[8,448,448]{1,2,0:T(8,128)S(1)}, u32[]{:S(2)}, u32[]{:S(2)}) %collective-permute-start.1) | collective-permute-done | bytes 6422560 | tf_op jit(solution)/shard_map/ppermute | solution.py:63
  799.9 7.9 add.113
  809.4 316.0 %collective-permute-done.2 = f32[8,448,448]{1,2,0:T(8,128)} collective-permute-done((f32[8,448,448]{1,2,0:T(8,128)}, f32[8,448,448]{1,2,0:T(8,128)}, u32[]{:S(2)}, u32[]{:S(2)}) %collective-permute-start.2) | collective-permute-done | bytes 6422560 | tf_op jit(solution)/shard_map/ppermute | solution.py:63
  1125.4 10.0 add.114
  1135.4 8.9 copy.102
  1154.4 93.8 %custom-call.34 = f32[8,128,128]{2,1,0:T(8,128)S(1)} custom-call(f32[8,128,128]{2,1,0:T(8,128)S(1)} %cholesky.281), custom_call_target="Cholesky" | custom-call | tf_op jit(solution)/shard_map/jit(cholesky)/cholesky | solution.py:18
  1252.2 79.2 %custom-call.35 = f32[8,1,128,128]{2,3,1,0:T(8,128)} custom-call(f32[8,1,128,128]{3,2,1,0:T(8,128)S(1)} %select_bitcast_fusion.2), custom_call_target="InvertDiagBlocksLowerTriangular" | custom-call | tf_op jit(solution)/shard_map/jit(cholesky)/cholesky | solution.py:18
  1339.1 94.0 %custom-call.36 = f32[8,128,128]{2,1,0:T(8,128)S(1)} custom-call(f32[8,128,128]{2,1,0:T(8,128)S(1)} %cholesky.285), custom_call_target="Cholesky" | custom-call | tf_op jit(solution)/shard_map/jit(cholesky)/cholesky | solution.py:18
  1434.0 79.2 %custom-call.37 = f32[8,1,128,128]{2,3,1,0:T(8,128)} custom-call(f32[8,1,128,128]{3,2,1,0:T(8,128)S(1)} %get-tuple-element.154), custom_call_target="InvertDiagBlocksLowerTriangular" | custom-call | tf_op jit(solution)/shard_map/jit(cholesky)/cholesky | solution.py:18
  1520.9 95.4 %custom-call.38 = f32[8,128,128]{2,1,0:T(8,128)} custom-call(f32[8,128,128]{2,1,0:T(8,128)} %cholesky.290), custom_call_target="Cholesky" | custom-call | tf_op jit(solution)/shard_map/jit(cholesky)/cholesky | solution.py:18
  1618.6 79.4 %custom-call.39 = f32[8,1,128,128]{2,3,1,0:T(8,128)S(1)} custom-call(f32[8,1,128,128]{3,2,1,0:T(8,128)} %get-tuple-element.152), custom_call_target="InvertDiagBlocksLowerTriangular" | custom-call | tf_op jit(solution)/shard_map/jit(cholesky)/cholesky | solution.py:18
  1701.9 46.9 %custom-call.40 = f32[8,64,64]{2,1,0:T(8,128)S(1)} custom-call(f32[8,64,64]{2,1,0:T(8,128)S(1)} %slice_subtract_fusion.2), custom_call_target="Cholesky" | custom-call | tf_op jit(solution)/shard_map/jit(cholesky)/cholesky | solution.py:18
  1757.2 12.6 while.16
  1773.1 316.1 %custom-call.41 = f32[8,4,128,128]{2,3,1,0:T(8,128)} custom-call(f32[8,4,128,128]{3,2,1,0:T(8,128)} %pad_maximum_fusion.1), custom_call_target="InvertDiagBlocksLowerTriangular" | custom-call | tf_op jit(solution)/shard_map/triangular_solve | solution.py:19
  2102.1 71.9 %all-gather.5.cloned.1.call-done = bf16[56,128,448]{2,1,0:T(8,128)(2,1)} async-done(((bf16[56,16,448]{2,1,0:T(8,128)(2,1)}), bf16[56,128,448]{2,1,0:T(8,128)(2,1)}) %all-gather.5.cloned.1.call-update) | async-done | bytes 6422544 | tf_op jit(solution)/shard_map/all_gather | solution.py:67
  2174.0 17.3 while.15
  2194.5 137.2 %all-reduce.10.cloned.1.call-done = (bf16[4,896,448]{1,2,0:T(8,128)(2,1)}, bf16[4,896,448]{1,2,0:T(8,128)(2,1)}) async-done(((bf16[4,896,448]{1,2,0:T(8,128)(2,1)}, bf16[4,896,448]{1,2,0:T(8,128)(2,1)}), (bf16[4,896,448]{1,2,0:T(8,128)(2,1)}, bf16[4,896,448]{1,2,0:T(8,128)(2,1)})) %all-reduce.10.cloned.1.call-update) | async-done | bytes 6422544 | tf_op jit(solution)/shard_map/psum | solution.py:14
  2331.8 7.4 fusion.50
  (104 shorter events, 106.6 us)
Async XLA Ops:
  7.2 365.2 %copy-start = (bf16[3584,448]{0,1:T(8,128)(2,1)S(1)}, bf16[3584,448]{0,1:T(8,128)(2,1)}, u32[]{:S(2)}) copy-start(bf16[3584,448]{0,1:T(8,128)(2,1)} %param.9) | copy-start | bytes 9633796
  7.2 360.2 %all-reduce.8.cloned.1.call-start = ((), (), s32[]{:S(2)}) async-start(), calls=%async_computation.4 | async-start | bytes 29360128
  70.4 0.7 copy-start.10
  70.4 380.5 %all-gather.3.cloned.1.call-start = ((), (), s32[]{:S(2)}) async-start(), calls=%async_computation.2 | async-start | bytes 9175040 | tf_op jit(solution)/shard_map/all_gather | solution.py:54
  371.8 230.4 %reduce-scatter.2.cloned.1.call-start = ((), (), s32[]{:S(2)}) async-start(), calls=%async_computation.1 | async-start | bytes 16515072 | tf_op jit(solution)/shard_map/reduce_scatter | solution.py:44
  431.2 0.7 copy-start.9
  431.2 1742.8 %all-gather.5.cloned.1.call-start = ((), (), s32[]{:S(2)}) async-start(), calls=%async_computation.3 | async-start | bytes 8257536 | tf_op jit(solution)/shard_map/all_gather | solution.py:67
  619.9 11.9 collective-permute-start
  639.6 160.2 %collective-permute-start.1 = (f32[8,448,448]{1,2,0:T(8,128)}, f32[8,448,448]{1,2,0:T(8,128)S(1)}, u32[]{:S(2)}, u32[]{:S(2)}) collective-permute-start(f32[8,448,448]{1,2,0:T(8,128)} %add.112), channel_id=1, source_target_pairs={{0,2},{1,3},{2,0},{3,1},{4,6},{5,7},{6,4},{7,5},{8,10},{9,11},{10,... | collective-permute-start | bytes 19267592 | tf_op jit(solution)/shard_map/ppermute | solution.py:63
  807.8 317.7 %collective-permute-start.2 = (f32[8,448,448]{1,2,0:T(8,128)}, f32[8,448,448]{1,2,0:T(8,128)}, u32[]{:S(2)}, u32[]{:S(2)}) collective-permute-start(f32[8,448,448]{1,2,0:T(8,128)} %add.113), channel_id=1, source_target_pairs={{0,4},{1,5},{2,6},{3,7},{4,0},{5,1},{6,2},{7,3},{8,12},{9,13},{10,... | collective-permute-start | bytes 19267592 | tf_op jit(solution)/shard_map/ppermute | solution.py:63
  1151.4 2.9 copy-start.3
  1248.2 4.0 copy-start.5
  1337.9 1.1 copy-start.4
  1433.0 80.2 %copy-start.7 = (f32[8,128,128]{2,1,0:T(8,128)}, f32[8,128,128]{2,1,0:T(8,128)S(1)}, u32[]{:S(2)}) copy-start(f32[8,128,128]{2,1,0:T(8,128)S(1)} %custom-call.36) | copy-start | bytes 1572868
  1513.2 103.1 %copy-start.6 = (f32[8,128,128]{2,1,0:T(8,128)S(1)}, f32[8,128,128]{2,1,0:T(8,128)}, u32[]{:S(2)}) copy-start(f32[8,128,128]{2,1,0:T(8,128)} %copy-done.5) | copy-start | bytes 1572868
  1754.2 2.9 copy-start.2
  2089.1 4.1 copy-start.8
  2102.1 229.7 %all-reduce.10.cloned.1.call-start = ((), (), s32[]{:S(2)}) async-start(), calls=%async_computation.5 | async-start | bytes 12845056 | tf_op jit(solution)/shard_map/psum | solution.py:14
  2331.8 7.4 copy-start.1
Sparse Core Ops, SparseCore 0:
  70.6 296.7 all-reduce.7
  371.9 78.9 all-gather.2
  453.2 148.9 reduce-scatter.1
  2102.2 71.7 all-gather.4
  2194.6 137.0 all-reduce.9
